TPU v7x, 128 devices: a whole 4x4x4 slice. The times are simulated.
128 devices in a mesh: tgt: 16 (over z_lo, y, core), src: 8 (over x, z_hi).
Axes of the slice: x: 4, y: 4, z: 4 (z_hi: 2, z_lo: 2; z = z_hi * 2 + z_lo), core: 2. Of those that a mesh axis runs over, the one named last changes fastest.
Arguments:
- targets: float32 [16, 64, 4096], P('tgt'), may hold values from -8 to 8
- sources: float32 [16, 64, 4096], P('src', 'tgt'), may hold values from -8 to 8
- occupations: float32 [16], P('src'), may hold values from 0.2 to 2
Outputs:
- exchange_term: float32 [16, 64, 4096], P('tgt', 'src')
All inputs are finite; a program needn't handle non-finite values.
Results may differ from a plain program's by a relative error of at most 0.000076.
Values sent between devices are 32-bit elements; how exact they have to be, the bound alone decides.
No kernel may reach another device: no remote copies, remote signals or barrier semaphores. Data moves between devices by JAX's collectives and lax.ppermute only.
A program may use at most 64 MiB of HBM per device.

v0:
```python
import math

import jax
import jax.numpy as jnp
from jax import lax
from jax.sharding import PartitionSpec as P

highest = lax.Precision.HIGHEST


def joined_along(tiles, dim):
    dims = list(tiles.shape[1:])
    dims[dim] *= tiles.shape[0]
    return jnp.moveaxis(tiles, 0, dim).reshape(dims)


def sent_to_all(shard, axis):
    copies = jnp.broadcast_to(shard, (lax.axis_size(axis), *shard.shape))
    return lax.all_to_all(copies, axis, split_axis=0, concat_axis=0, tiled=True)


def collect(shard, axis, dim):
    return joined_along(sent_to_all(shard, axis), dim)


def cut_along(shard, dim, length):
    before, after = (shard.shape[:dim], shard.shape[dim + 1 :])
    return jnp.moveaxis(shard.reshape(*before, length, -1, *after), dim, 0)


def summed_on_arrival(shard, axis, dim):
    tiles = cut_along(shard, dim, lax.axis_size(axis))
    arrived = lax.all_to_all(tiles, axis, split_axis=0, concat_axis=0, tiled=True)
    return arrived.sum(axis=0)


def dft_tables(size):
    index = jnp.arange(size, dtype=jnp.int32)
    phase = index[:, None] * index[None, :] % size
    angle = phase.astype(jnp.float32) * (2.0 * math.pi / size)
    return (jnp.cos(angle), jnp.sin(angle))


def kernel_packed(size):
    freq = ((jnp.arange(size, dtype=jnp.int32) + size // 2) % size - size // 2).astype(jnp.float32)
    square = freq[:, None, None] ** 2 + freq[None, :, None] ** 2 + freq[None, None, :] ** 2
    base = 16.0 / (square + 0.25)
    return jnp.concatenate([base, base], axis=-1)


def swapped(field, size):
    signs = jnp.concatenate([jnp.ones((size,), jnp.float32), -jnp.ones((size,), jnp.float32)])
    return jnp.roll(field, size, axis=-1) * signs


def along_rows(field, cos_table, sin_table, direction):
    other = swapped(field, cos_table.shape[0])
    first = jnp.einsum("ky,txyc->txkc", cos_table, field, precision=highest)
    second = jnp.einsum("ky,txyc->txkc", sin_table, other, precision=highest)
    return first + direction * second


def along_planes(field, cos_table, sin_table, direction):
    other = swapped(field, cos_table.shape[0])
    first = jnp.einsum("kx,txyc->tkyc", cos_table, field, precision=highest)
    second = jnp.einsum("kx,txyc->tkyc", sin_table, other, precision=highest)
    return first + direction * second


def forward_depth(field, cos_table, sin_table):
    matrix = jnp.concatenate([cos_table, -sin_table], axis=1)
    return jnp.dot(field, matrix, precision=highest)


def inverse_depth(field, cos_table, sin_table):
    size = cos_table.shape[0]
    matrix = jnp.concatenate([cos_table, -sin_table], axis=0) / float(size**3)
    return jnp.dot(field, matrix, precision=highest)


def whole_term(targets, source_field, weight, cos_table, sin_table, kernel):
    size = targets.shape[1]
    count = targets.shape[0]
    pair = (targets * source_field[None]).reshape(count, size, size, size)
    spectrum = along_rows(forward_depth(pair, cos_table, sin_table), cos_table, sin_table, 1.0)
    spectrum = along_planes(spectrum, cos_table, sin_table, 1.0) * kernel[None]
    back = along_rows(
        along_planes(spectrum, cos_table, sin_table, -1.0), cos_table, sin_table, -1.0
    )
    potential = inverse_depth(back, cos_table, sin_table)
    return weight * source_field[None] * potential.reshape(count, size, size * size)


def on_device(targets, sources, occupations):
    size = targets.shape[1]
    cos_table, sin_table = dft_tables(size)
    kernel = kernel_packed(size)
    whole = collect(sources, "tgt", 1)
    total = jnp.zeros(targets.shape, jnp.float32)
    for source_index in range(whole.shape[0]):
        total = total - whole_term(
            targets, whole[source_index], occupations[source_index], cos_table, sin_table, kernel
        )
    return summed_on_arrival(total, "src", 1)


def solution(mesh):
    return jax.shard_map(
        on_device,
        mesh=mesh,
        in_specs=(P("tgt", None, None), P("src", "tgt", None), P("src")),
        out_specs=P("tgt", "src", None),
        check_vma=False,
    )
```

profile of v0, /device:TPU:8, one launch (start us, length us, event | category | flops | bytes accessed | tf_op | source)
XLA Modules:
  0.0 179.2 jit_solution(7201226911557309233)
XLA Ops:
  0.0 2.7 %broadcast_in_dim.7 = f32[16,2,4,4096]{3,2,1,0:T(4,128)} broadcast(f32[2,4,4096]{2,1,0:T(4,128)} %param.4), dimensions={1,2,3} | broadcast | bytes 2228224 | tf_op jit(solution)/shard_map/broadcast_in_dim | solution.py:18
  2.7 6.4 %all-to-all-start = ((f32[16,2,4,4096]{3,2,1,0:T(4,128)}), f32[16,2,4,4096]{3,2,1,0:T(4,128)S(1)}, u32[]{:S(2)}, u32[]{:S(2)}) async-start(f32[16,2,4,4096]{3,2,1,0:T(4,128)} %broadcast_in_dim.7), calls=%async_computation | async-start | bytes 4194304 | tf_op jit(solution)/shard_map/all_to_all | solution.py:19
  11.7 26.0 %all-to-all-done = f32[16,2,4,4096]{3,2,1,0:T(4,128)S(1)} async-done(((f32[16,2,4,4096]{3,2,1,0:T(4,128)}), f32[16,2,4,4096]{3,2,1,0:T(4,128)S(1)}, u32[]{:S(2)}, u32[]{:S(2)}) %all-to-all-start) | async-done | bytes 2097184 | tf_op jit(solution)/shard_map/all_to_all | solution.py:19
  37.6 3.7 %broadcast_multiply_fusion.1 = (f32[1,16,4,4096]{3,2,0,1:T(4,128)}, f32[1,16,4,4096]{3,2,0,1:T(4,128)}, f32[1,16,4,4096]{3,2,0,1:T(4,128)S(1)}, f32[1,16,4,4096]{3,2,0,1:T(4,128)}) fusion(f32[]{:T(128)} %bitcast, f32[2,16,4,4096]{3,2,0,1:T(4,128)S(1)} %bitcast.183, f32[]{:T(128)} %bitcast.38), kind=kLoop, calls=%fused_computation.89 | loop fusion | flops 524288 | bytes 6291464 | tf_op jit(solution)/shard_map/mul | solution.py:91
  55.2 2.8 %slice_bitcast_fusion.5 = (f32[64,64,64]{2,1,0:T(8,128)}, f32[64,64,64]{2,1,0:T(8,128)}) fusion(f32[1,64,64,128]{3,2,1,0:T(8,128)S(1)} %bitcast.177), kind=kLoop, calls=%fused_computation.5 | loop fusion | bytes 4194304 | tf_op jit(solution)/shard_map/jit(_roll_static)/concatenate | solution.py:53
  60.2 3.4 %fusion.49 = f32[64,64,128]{2,1,0:T(8,128)S(1)} fusion(f32[64,64,64]{2,1,0:T(8,128)} %reshape.337, f32[64,64]{0,1:T(8,128)S(1)} %get-tuple-element.36, f32[64,64]{0,1:T(8,128)S(1)} %get-tuple-element.35), kind=kOutput, calls=%fused_computation.92 | convolution fusion | flops 402661376 | bytes 3178496 | tf_op jit(solution)/shard_map/dot_general | solution.py:72
  66.7 2.7 %fusion.39 = f32[64,128,64]{1,2,0:T(8,128)S(1)} fusion(f32[64,128,64]{1,2,0:T(8,128)S(1)} %fusion.70, f32[64,64,64]{2,1,0:T(8,128)S(1)} %get-tuple-element.18, f32[64,64,64]{2,1,0:T(8,128)S(1)} %get-tuple-element.17, f32[128]{0:T(128)S(1)} %copy-done.5), kind=kOutput, calls=%fused_computation.77 | convolution fusion | flops 404283392 | bytes 6291968 | tf_op jit(solution)/shard_map/ky,txyc->txkc/dot_general | solution.py:59
  72.8 3.4 %fusion.23 = f32[64,128,64]{1,2,0:T(8,128)S(1)} fusion(f32[64,64,128]{2,1,0:T(8,128)S(1)} %get-tuple-element.34), kind=kOutput, calls=%fused_computation.55 | convolution fusion | flops 402710528 | bytes 4194304 | tf_op jit(solution)/shard_map/kx,txyc->tkyc/dot_general | solution.py:66
  76.2 3.8 %fusion.34 = f32[64,128,64]{1,2,0:T(8,128)S(1)} fusion(f32[64,64,128]{2,1,0:T(8,128)S(1)} %get-tuple-element.33), kind=kOutput, calls=%fused_computation.71 | convolution fusion | flops 402710528 | bytes 4194304 | tf_op jit(solution)/shard_map/kx,txyc->tkyc/dot_general | solution.py:66
  80.0 3.4 %fusion.25 = f32[64,128,64]{1,2,0:T(8,128)S(1)} fusion(f32[64,64,128]{2,1,0:T(8,128)S(1)} %bitcast.178), kind=kOutput, calls=%fused_computation.57 | convolution fusion | flops 402710528 | bytes 4194304 | tf_op jit(solution)/shard_map/kx,txyc->tkyc/dot_general | solution.py:65
  83.4 3.4 %fusion.36 = f32[64,128,64]{1,2,0:T(8,128)S(1)} fusion(f32[64,64,128]{2,1,0:T(8,128)S(1)} %bitcast.180), kind=kOutput, calls=%fused_computation.73 | convolution fusion | flops 402710528 | bytes 4194304 | tf_op jit(solution)/shard_map/kx,txyc->tkyc/dot_general | solution.py:65
  86.8 5.1 %bitcast_multiply_fusion.1 = (f32[1,64,64,128]{3,2,1,0:T(8,128)S(1)}, f32[1,64,64,128]{3,2,1,0:T(8,128)S(1)}) fusion(f32[64,128,64]{1,2,0:T(8,128)S(1)} %fusion.34, f32[64,128,64]{1,2,0:T(8,128)S(1)} %fusion.36, f32[64,64,64]{2,1,0:T(8,128)S(1)} %copy-done.1, f32[64,128,64]{1,2,0:T(8,128)S(1)} %fusion.23, f32[64,128,64]{1,2,0:T(8,128)S(1)} %fusion.25), kind=kLoop, calls=%fused_computation.42 | loop fusion | flops 2621440 | bytes 13631488 | tf_op jit(solution)/shard_map/mul | solution.py:86
  94.7 3.4 %fusion.30 = f32[64,128,64]{1,2,0:T(8,128)S(1)} fusion(f32[64,64,128]{2,1,0:T(8,128)S(1)} %get-tuple-element.31), kind=kOutput, calls=%fused_computation.66 | convolution fusion | flops 402710528 | bytes 4194304 | tf_op jit(solution)/shard_map/kx,txyc->tkyc/dot_general | solution.py:66
  98.1 3.4 %fusion.32 = f32[64,128,64]{1,2,0:T(8,128)S(1)} fusion(f32[64,64,128]{2,1,0:T(8,128)S(1)} %bitcast.176), kind=kOutput, calls=%fused_computation.68 | convolution fusion | flops 402710528 | bytes 4194304 | tf_op jit(solution)/shard_map/kx,txyc->tkyc/dot_general | solution.py:65
  103.9 5.1 %fusion.14 = f32[64,128,64]{1,2,0:T(8,128)S(1)} fusion(f32[64,128,64]{1,2,0:T(8,128)S(1)} %fusion.32, f32[64,128,64]{1,2,0:T(8,128)S(1)} %fusion.30), kind=kOutput, calls=%fused_computation.40 | convolution fusion | flops 403759104 | bytes 6291456 | tf_op jit(solution)/shard_map/ky,txyc->txkc/dot_general | solution.py:58
  109.1 3.4 %fusion.19 = f32[64,128,64]{1,2,0:T(8,128)S(1)} fusion(f32[64,64,128]{2,1,0:T(8,128)S(1)} %get-tuple-element.32), kind=kOutput, calls=%fused_computation.50 | convolution fusion | flops 402710528 | bytes 4194304 | tf_op jit(solution)/shard_map/kx,txyc->tkyc/dot_general | solution.py:66
  112.5 3.4 %fusion.21 = f32[64,128,64]{1,2,0:T(8,128)S(1)} fusion(f32[64,64,128]{2,1,0:T(8,128)S(1)} %bitcast.175), kind=kOutput, calls=%fused_computation.52 | convolution fusion | flops 402710528 | bytes 4194304 | tf_op jit(solution)/shard_map/kx,txyc->tkyc/dot_general | solution.py:65
  115.8 2.9 %fusion.47 = f32[1,64,64,128]{3,2,1,0:T(8,128)S(1)} fusion(f32[64,128,64]{1,2,0:T(8,128)S(1)} %fusion.19, f32[64,128,64]{1,2,0:T(8,128)S(1)} %fusion.21), kind=kLoop, calls=%fused_computation.87 | loop fusion | flops 1048576 | bytes 6291456 | tf_op jit(solution)/shard_map/add | solution.py:67
  118.7 6.4 %fusion.12 = f32[64,128,64]{1,2,0:T(8,128)} fusion(f32[64,128,64]{1,2,0:T(8,128)S(1)} %fusion.21, f32[64,128,64]{1,2,0:T(8,128)S(1)} %fusion.19), kind=kOutput, calls=%fused_computation.37 | convolution fusion | flops 403759104 | bytes 6291456 | tf_op jit(solution)/shard_map/ky,txyc->txkc/dot_general | solution.py:58
  128.5 2.6 %fusion.29 = f32[64,64,128]{2,0,1:T(8,128)S(1)} fusion(f32[64,128,64]{1,2,0:T(8,128)S(1)} %fusion.14, f32[64,128,64]{1,2,0:T(8,128)S(1)} %fusion.3), kind=kLoop, calls=%fused_computation.62 | loop fusion | flops 1048576 | bytes 6291456 | tf_op jit(solution)/shard_map/reshape.29
  131.1 4.5 %fusion.27 = f32[64,64,64]{2,1,0:T(8,128)} fusion(f32[64,64,128]{2,0,1:T(8,128)S(1)} %fusion.29, f32[64,64]{0,1:T(8,128)S(1)} %get-tuple-element.36, f32[64,64]{0,1:T(8,128)S(1)} %get-tuple-element.35), kind=kOutput, calls=%fused_computation.59 | convolution fusion | flops 402669568 | bytes 3178496 | tf_op jit(solution)/shard_map/dot_general | solution.py:78
  138.6 2.6 %fusion.9 = f32[64,128,64]{1,2,0:T(8,128)S(1)} fusion(f32[64,64,64]{2,1,0:T(8,128)S(1)} %get-tuple-element.20, f32[64,64,64]{2,1,0:T(8,128)S(1)} %get-tuple-element.19, f32[128]{0:T(128)S(1)} %copy-done.5), kind=kOutput, calls=%fused_computation.34 | convolution fusion | flops 403759104 | bytes 4194816 | tf_op jit(solution)/shard_map/ky,txyc->txkc/dot_general | solution.py:59
  143.7 3.2 %fusion.16 = f32[64,64,64]{2,1,0:T(8,128)S(1)} fusion(f32[64,64,128]{2,0,1:T(8,128)S(1)} %fusion.18, f32[64,64]{0,1:T(8,128)S(1)} %get-tuple-element.36, f32[64,64]{0,1:T(8,128)S(1)} %get-tuple-element.35), kind=kOutput, calls=%fused_computation.43 | convolution fusion | flops 402669568 | bytes 3178496 | tf_op jit(solution)/shard_map/dot_general | solution.py:78
  154.2 24.1 %all_to_all.10 = f32[8,1,8,4096]{3,2,1,0:T(8,128)S(1)} all-to-all(f32[8,1,8,4096]{3,2,1,0:T(8,128)S(1)} %fusion.40), channel_id=1, replica_groups=mesh['tgt'=16,'src'=8] {'src'}, dimensions={0} | all-to-all | bytes 2097152 | tf_op jit(solution)/shard_map/all_to_all | solution.py:33
  (46 shorter events, 47.0 us)
Async XLA Ops:
  2.7 6.4 %copy-start.6 = (f32[2]{0:T(128)S(1)}, f32[2]{0:T(128)}, u32[]{:S(2)}) copy-start(f32[2]{0:T(128)} %param.5) | copy-start | bytes 28
  2.7 35.0 %all-to-all-start = ((f32[16,2,4,4096]{3,2,1,0:T(4,128)}), f32[16,2,4,4096]{3,2,1,0:T(4,128)S(1)}, u32[]{:S(2)}, u32[]{:S(2)}) async-start(f32[16,2,4,4096]{3,2,1,0:T(4,128)} %broadcast_in_dim.7), calls=%async_computation | async-start | bytes 4194304 | tf_op jit(solution)/shard_map/all_to_all | solution.py:19
  51.7 0.8 copy-start.5
  69.3 1.6 copy-start.2
  69.4 2.2 %copy-start.3 = (f32[64,64,64]{2,1,0:T(8,128)S(1)}, f32[64,64,64]{2,1,0:T(8,128)}, u32[]{:S(2)}) copy-start(f32[64,64,64]{2,1,0:T(8,128)} %get-tuple-element.24) | copy-start | bytes 3145732
  83.4 3.4 %copy-start.1 = (f32[64,64,64]{2,1,0:T(8,128)S(1)}, f32[64,64,64]{2,1,0:T(8,128)}, u32[]{:S(2)}) copy-start(f32[64,64,64]{2,1,0:T(8,128)} %add_divide_fusion) | copy-start | bytes 3145732
  138.6 2.6 %copy-start = (f32[64,128,64]{1,2,0:T(8,128)S(1)}, f32[64,128,64]{1,2,0:T(8,128)}, u32[]{:S(2)}) copy-start(f32[64,128,64]{1,2,0:T(8,128)} %fusion.12) | copy-start | bytes 6291460
  148.5 4.2 %copy-start.4 = (f32[8,1,8,4096]{3,2,0,1:T(8,128)S(1)}, f32[8,1,8,4096]{3,2,0,1:T(8,128)}, u32[]{:S(2)}) copy-start(f32[8,1,8,4096]{3,2,0,1:T(8,128)} %reshape.348) | copy-start | bytes 3145732
where the time goes:
time: 183 us; the launch traced here: 179 us
  matrix products  66.8 us (37%)
  other arithmetic  28 us (15%)
  local copies, waits for them, and re-layouts  27.5 us (15%)
  waiting for transfers between devices  26 us (14%)
  blocking collectives  24.1 us (13%)
  starting transfers between devices  6.42 us (4%)
    all_to_all x1, waiting for transfers between devices, sent_to_all(): return lax.all_to_all(copies, axis, split_axis=0, concat_axis=0, tiled=True)  26 us
    all_to_all x1, blocking collectives, summed_on_arrival(): lax.all_to_all(tiles, axis, split_axis=0, concat_axis=0, tiled=True)  24.1 us
    dot_general x4, matrix products, along_rows(): first = jnp.einsum('ky,txyc->txkc', cos_table, field, precision=highest)  15.9 us
    dot_general x4, matrix products, along_planes(): second = jnp.einsum('kx,txyc->tkyc', sin_table, other, precision=highest)  13.9 us
    dot_general x4, matrix products, along_planes(): first = jnp.einsum('kx,txyc->tkyc', cos_table, field, precision=highest)  13.5 us
    dot_general x4, matrix products, along_rows(): second = jnp.einsum('ky,txyc->txkc', sin_table, other, precision=highest)  10.4 us
    concatenate x8, local copies, waits for them, and re-layouts, swapped(): return jnp.roll(field, size, axis=-1) * signs  8.4 us
    dot_general x2, matrix products, inverse_depth(): return jnp.dot(field, matrix, precision=highest)  7.78 us
  transfers between devices with their start and end apart: 1, of which 1 were waited for; matrix products, arithmetic and copies ran while one was open for 1% of the time, Pallas kernels for 0%

commit v1 on v0

v1 whole, which is shorter than its diff:
```python
import functools

import jax
import jax.numpy as jnp
import numpy as np
from jax import lax
from jax.experimental import pallas as pl
from jax.experimental.pallas import tpu as pltpu
from jax.sharding import PartitionSpec as P

N = 64
H = 32
L = 128
PAIRS = N // 2


def real_basis():
    n = np.arange(N)
    rows = [np.ones(N)]
    for k in range(1, N // 2):
        rows.append(np.sqrt(2.0) * np.cos(2 * np.pi * k * n / N))
    rows.append((-1.0) ** n)
    for k in range(1, N // 2):
        rows.append(np.sqrt(2.0) * np.sin(2 * np.pi * k * n / N))
    freq = np.array(list(range(0, N // 2 + 1)) + list(range(1, N // 2)), np.float64)
    return np.array(rows) / np.sqrt(N), freq


def halves(table):
    high = table.astype(jnp.bfloat16)
    low = (table - high.astype(np.float64)).astype(jnp.bfloat16)
    return high, low


def left_table(matrix):
    high, low = halves(matrix)
    return np.concatenate([high, high, low, low], axis=1)


def right_table(matrix):
    block = np.zeros((L, L))
    block[:N, :N] = matrix
    block[N:, N:] = matrix
    high, low = halves(block)
    both = np.concatenate([high, low], axis=1)
    return np.concatenate([both, both], axis=0)


BASIS, FREQ = real_basis()
ORDER = np.concatenate([np.arange(0, N, 2), np.arange(1, N, 2)])
BASIS_Y = BASIS[:, ORDER]


def split(value):
    high = value.astype(jnp.bfloat16)
    low = (value - high.astype(jnp.float32)).astype(jnp.bfloat16)
    return high, low


def stacked(value):
    high, low = split(value)
    return jnp.concatenate([high, low, high, low], axis=0)


def dot(left, right):
    return jnp.dot(left, right, preferred_element_type=jnp.float32)


def from_left(table, first, second):
    both = jnp.concatenate([stacked(first), stacked(second)], axis=1)
    out = dot(table, both)
    return out[:, :L], out[:, L:]


def from_right(value, table):
    high, low = split(value)
    out = dot(jnp.concatenate([high, low], axis=1), table)
    return out[:, :L] + out[:, L:]


def exchange_kernel(s_ref, t_ref, k_ref, w_ref, ly, lx, ix, iy, rz, qz, out_ref, one, two):
    def forward(i, _):
        fields = []
        for e in range(2):
            x = 2 * i + e
            fields.append(from_right(t_ref[x] * s_ref[x], rz[...]))
        a, b = from_left(ly[...], *fields)
        one[pl.ds(pl.multiple_of(2 * i * N, N), N), :] = a
        one[pl.ds(pl.multiple_of((2 * i + 1) * N, N), N), :] = b
        return 0

    lax.fori_loop(0, PAIRS, forward, 0, unroll=4)

    def middle(i, _):
        first = one[pl.ds(2 * i, N, stride=N), :]
        second = one[pl.ds(2 * i + 1, N, stride=N), :]
        a, b = from_left(lx[...], first, second)
        a = a * k_ref[2 * i]
        b = b * k_ref[2 * i + 1]
        a, b = from_left(ix[...], a, b)
        two[pl.ds(2 * i, N, stride=N), :] = a
        two[pl.ds(2 * i + 1, N, stride=N), :] = b
        return 0

    lax.fori_loop(0, PAIRS, middle, 0, unroll=4)

    lane = lax.broadcasted_iota(jnp.int32, (H, L), 1) < N

    def backward(i, _):
        first = two[pl.ds(pl.multiple_of(2 * i * N, N), N), :]
        second = two[pl.ds(pl.multiple_of((2 * i + 1) * N, N), N), :]
        fields = from_left(iy[...], first, second)
        for e in range(2):
            x = 2 * i + e
            v = from_right(fields[e], qz[...]) * s_ref[x] * w_ref[...]
            even, odd = v[:H], v[H:]
            kept = jnp.where(lane, even, odd)
            moved = jnp.where(lane, odd, even)
            out_ref[x] = kept + pltpu.roll(moved, N, axis=1)
        return 0

    lax.fori_loop(0, PAIRS, backward, 0, unroll=4)


def exchange(s, t, k, w):
    tables = (
        left_table(BASIS_Y),
        left_table(BASIS),
        left_table(BASIS.T),
        left_table(BASIS_Y.T),
        right_table(BASIS.T),
        right_table(BASIS),
    )
    return pl.pallas_call(
        exchange_kernel,
        out_shape=jax.ShapeDtypeStruct((N, H, L), jnp.float32),
        scratch_shapes=[pltpu.VMEM((N * N, L), jnp.float32), pltpu.VMEM((N * N, L), jnp.float32)],
        name="exchange",
    )(s, t, k, w, *[jnp.asarray(v) for v in tables])


def kernel_grid():
    freq = jnp.asarray(FREQ, jnp.float32) ** 2
    square = freq[:, None, None] + freq[None, :, None] + freq[None, None, :]
    base = 16.0 / (square + 0.25)
    return jnp.concatenate([base, base], axis=-1)


def on_device(targets, sources, occupations):
    w = -jnp.repeat(occupations, N).reshape(1, L)
    packed = sources.reshape(2, 4, H, 2, N).transpose(1, 3, 2, 0, 4).reshape(4, N, L)
    copies = jnp.broadcast_to(packed, (16, 4, N, L))
    whole = lax.all_to_all(copies, "tgt", split_axis=0, concat_axis=0, tiled=True)
    whole = whole.reshape(N, N, L)
    t = targets.reshape(N, H, 2, N).transpose(0, 2, 1, 3).reshape(N, N, N)
    t = jnp.concatenate([t, t], axis=-1)
    part = exchange(whole, t, kernel_grid(), w)
    tiles = part.reshape(8, 8, H, L)
    arrived = lax.all_to_all(tiles, "src", split_axis=0, concat_axis=0, tiled=True)
    return arrived.sum(axis=0).reshape(1, 8, H * L)


def solution(mesh):
    return jax.shard_map(
        on_device,
        mesh=mesh,
        in_specs=(P("tgt", None, None), P("src", "tgt", None), P("src")),
        out_specs=P("tgt", "src", None),
        check_vma=False,
    )
```

time: 183 us -> 86 us (0.47); the launches traced: 179 us -> 85.7 us
  matrix products: 66.8 us -> 0 us
  other arithmetic: 28 us -> 3.88 us
  Pallas kernels: 0 us -> 22.5 us
  local copies, waits for them, and re-layouts: 27.5 us -> 7.77 us
  waiting for transfers between devices: 26 us -> 20.8 us
    dot_general x20 -> x0, matrix products: 66.8 us -> none  [the longest x4 15.9 us: along_rows(): first = jnp.einsum('ky,txyc->txkc', cos_table, field, precision=highest)]
    pallas_call x0 -> x1, Pallas kernels: none -> 22.5 us  [exchange(): pl.pallas_call(exchange_kernel, out_shape=jax.ShapeDtypeStruct((N, H, L),...]
    mul x5 -> x0, other arithmetic: 13.5 us -> none  [the longest x1 5.1 us: whole_term(): spectrum = along_planes(spectrum, cos_table, sin_table, 1.0) * kernel[None]]
    concatenate x8 -> x0, local copies, waits for them, and re-layouts: 8.4 us -> none  [swapped(): return jnp.roll(field, size, axis=-1) * signs]
    add x3 -> x1, other arithmetic: 5.4 us -> 0.07 us  [kernel_grid(): square = freq[:, None, None] + freq[None, :, None] + freq[None, None, :]]
    all_to_all x1, waiting for transfers between devices: 26 us -> 20.8 us  [on_device(): lax.all_to_all(copies, 'tgt', split_axis=0, concat_axis=0, tiled=True)]
    another operation x2 -> x0, other arithmetic: 5.04 us -> none
    another operation x2 -> x0, local copies, waits for them, and re-layouts: 4.37 us -> none
  transfers between devices with their start and end apart: 1 -> 1, of which waited for: 1 -> 1; matrix products, arithmetic and copies ran while one was open for 1% -> 9% of each run, Pallas kernels for 0% -> 0%
where the time goes in v1:
time: 86 us; the launch traced here: 85.7 us
  blocking collectives  24.3 us (28%)
  Pallas kernels  22.5 us (26%)
  waiting for transfers between devices  20.8 us (24%)
  local copies, waits for them, and re-layouts  7.77 us (9%)
  starting transfers between devices  6.42 us (7%)
  other arithmetic  3.88 us (5%)
    all_to_all x1, blocking collectives, on_device(): lax.all_to_all(tiles, 'src', split_axis=0, concat_axis=0, tiled=True)  24.3 us
    pallas_call x1, Pallas kernels, exchange(): pl.pallas_call(exchange_kernel, out_shape=jax.ShapeDtypeStruct((N, H, L),...  22.5 us
    all_to_all x1, waiting for transfers between devices, on_device(): lax.all_to_all(copies, 'tgt', split_axis=0, concat_axis=0, tiled=True)  20.8 us
    all_to_all x1, starting transfers between devices, on_device(): lax.all_to_all(copies, 'tgt', split_axis=0, concat_axis=0, tiled=True)  6.42 us
    concatenate x1, other arithmetic, on_device(): t = jnp.concatenate([t, t], axis=-1)  3.11 us
    reshape x2, local copies, waits for them, and re-layouts, on_device(): t = targets.reshape(N, H, 2, N).transpose(0, 2, 1, 3).reshape(N, N, N)  3.11 us
  transfers between devices with their start and end apart: 1, of which 1 were waited for; matrix products, arithmetic and copies ran while one was open for 9% of the time, Pallas kernels for 0%

profile of v1, /device:TPU:8, one launch (start us, length us, event | category | flops | bytes accessed | tf_op | source)
XLA Modules:
  0.0 85.7 jit_solution(13761107737581766096)
XLA Ops:
  0.0 1.1 %reshape.67 = f32[2,4,32,2,64]{4,3,2,1,0:T(2,128)S(1)} reshape(f32[2,4,4096]{2,1,0:T(4,128)} %param.11) | data formatting | bytes 262144 | tf_op jit(solution)/shard_map/reshape | solution.py:151
  1.1 0.2 copy.17
  1.3 0.2 reshape.68
  1.5 1.6 %broadcast_in_dim.4 = f32[16,4,64,128]{3,2,1,0:T(8,128)} broadcast(f32[4,64,128]{2,1,0:T(8,128)S(1)} %reshape.68), dimensions={1,2,3} | broadcast | bytes 2228224 | tf_op jit(solution)/shard_map/broadcast_in_dim | solution.py:152
  3.1 0.0 copy-start.1
  3.1 6.4 %all-to-all-start = ((f32[16,4,64,128]{3,2,1,0:T(8,128)}), f32[16,4,64,128]{3,2,1,0:T(8,128)}, u32[]{:S(2)}, u32[]{:S(2)}) async-start(f32[16,4,64,128]{3,2,1,0:T(8,128)} %broadcast_in_dim.4), calls=%async_computation | async-start | bytes 4194304 | tf_op jit(solution)/shard_map/all_to_all | solution.py:153
  9.5 0.0 copy-done.1
  9.5 1.5 %reshape.70 = f32[64,32,2,64]{3,2,1,0:T(2,128)S(1)} reshape(f32[1,64,4096]{2,1,0:T(8,128)S(1)} %copy-done.1) | data formatting | bytes 2097152 | tf_op jit(solution)/shard_map/reshape | solution.py:155
  11.0 0.0 copy-start.3
  11.0 0.0 copy-start.2
  11.1 1.6 %copy.15 = f32[64,32,2,64]{3,1,2,0:T(8,128)} copy(f32[64,32,2,64]{3,2,1,0:T(2,128)S(1)} %reshape.70) | data formatting | bytes 2097152 | tf_op jit(solution)/shard_map/reshape | solution.py:155
  12.7 0.0 copy-done.3
  12.7 0.1 broadcast_in_dim.10
  12.7 0.6 neg.6.w_ref
  13.3 0.0 copy-done.2
  13.3 0.1 broadcast_add_fusion
  13.4 0.6 add_divide_fusion
  14.0 0.2 copy-done
  14.2 3.1 %pad_maximum_fusion = (f32[64,64,128]{2,1,0:T(8,128)}, f32[64,64,128]{2,1,0:T(8,128)}) fusion(f32[64,64,64]{2,1,0:T(8,128)S(1)} %bitcast.8, f32[64,64,64]{2,1,0:T(8,128)S(1)} %add_divide_fusion), kind=kLoop, calls=%fused_computation | loop fusion | flops 1048576 | bytes 6291456 | tf_op jit(solution)/shard_map/concatenate | solution.py:156
  17.4 20.8 %all-to-all-done = f32[16,4,64,128]{3,2,1,0:T(8,128)} async-done(((f32[16,4,64,128]{3,2,1,0:T(8,128)}), f32[16,4,64,128]{3,2,1,0:T(8,128)}, u32[]{:S(2)}, u32[]{:S(2)}) %all-to-all-start) | async-done | bytes 2097184 | tf_op jit(solution)/shard_map/all_to_all | solution.py:153
  38.2 22.5 %exchange.1 = f32[64,32,128]{2,1,0:T(8,128)} custom-call(f32[64,64,128]{2,1,0:T(8,128)} %bitcast.1.s_ref, f32[64,64,128]{2,1,0:T(8,128)} %get-tuple-element.5.t_ref, f32[64,64,128]{2,1,0:T(8,128)} %get-tuple-element.6.k_ref, f32[1,128]{1,0:T(1,128)} %neg.6.w_ref, bf16[64,256]{1,0:T(8,128)(2,1)} %constant.21.clone.ly, bf16[64,256]{1,0:T(8,128)(2,1)} %constant.22.clone.lx, ...), custom_call_target="tpu_custom_call" | custom-call | tf_op jit(solution)/shard_map/exchange/pallas_call | solution.py:134
  60.7 24.3 %all_to_all.10 = f32[8,8,32,128]{3,2,1,0:T(8,128)S(1)} all-to-all(f32[8,8,32,128]{3,2,1,0:T(8,128)} %bitcast.9), channel_id=1, replica_groups=mesh['tgt'=16,'src'=8] {'src'}, dimensions={0} | all-to-all | bytes 2097152 | tf_op jit(solution)/shard_map/all_to_all | solution.py:159
  84.9 0.1 reduce_sum.9
  85.0 0.7 reshape.73
  (2 shorter events, 0.0 us)
Async XLA Ops:
  3.1 6.4 %copy-start.1 = (f32[1,64,4096]{2,1,0:T(8,128)S(1)}, f32[1,64,4096]{2,1,0:T(8,128)}, u32[]{:S(2)}) copy-start(f32[1,64,4096]{2,1,0:T(8,128)} %param.10) | copy-start | bytes 3145732
  3.1 35.1 %all-to-all-start = ((f32[16,4,64,128]{3,2,1,0:T(8,128)}), f32[16,4,64,128]{3,2,1,0:T(8,128)}, u32[]{:S(2)}, u32[]{:S(2)}) async-start(f32[16,4,64,128]{3,2,1,0:T(8,128)} %broadcast_in_dim.4), calls=%async_computation | async-start | bytes 4194304 | tf_op jit(solution)/shard_map/all_to_all | solution.py:153
  11.0 1.6 %copy-start.3 = (f32[2]{0:T(128)S(1)}, f32[2]{0:T(128)}, u32[]{:S(2)}) copy-start(f32[2]{0:T(128)} %param.12) | copy-start | bytes 28
  11.0 2.3 %copy-start.2 = (f32[64]{0:T(128)S(1)}, f32[64]{0:T(128)}, u32[]{:S(2)}) copy-start(f32[64]{0:T(128)} %constant.30) | copy-start | bytes 772
  12.7 1.6 %copy-start = (f32[64,32,2,64]{3,1,2,0:T(8,128)S(1)}, f32[64,32,2,64]{3,1,2,0:T(8,128)}, u32[]{:S(2)}) copy-start(f32[64,32,2,64]{3,1,2,0:T(8,128)} %copy.15) | copy-start | bytes 3145732
